TPU v7x, 32 devices: a whole 2x2x4 slice. The times are simulated.
32 devices in a mesh: cores: 2 (over core), row: 4 (over y, x), vec: 4 (over z).
Axes of the slice: x: 2, y: 2, z: 4, core: 2. Of those that a mesh axis runs over, the one named last changes fastest.
Arguments:
- train_cores: float32 [4, 512, 256, 256], P('vec', 'cores', 'row'), may hold values from -0.01953125 to 0.01953125
- sketch: float32 [512, 128], P('cores'), may hold values from -6 to 6
- exit_sketch: float32 [256, 128], replicated, may hold values from -6 to 6
Outputs:
- rounded: float32 [4, 256, 256, 128], P('vec', 'cores', 'row')
- interface_bases: float32 [4, 512, 128], P('vec', 'cores')
- margins: float32 [4, 256, 512], P('vec', 'cores')
All inputs are finite; a program needn't handle non-finite values.
Results may differ from a plain program's by a relative error of at most 0.0003.
Values sent between devices are 32-bit elements; how exact they have to be, the bound alone decides.
No kernel may reach another device: no remote copies, remote signals or barrier semaphores. Data moves between devices by JAX's collectives and lax.ppermute only.
A program may use at most 192 MiB of HBM per device.

v0:
```python
import math
import jax
import jax.numpy as jnp
from jax import lax
from jax.sharding import PartitionSpec as P

MODE = 256


def broadcast(block, axis, holder):
    block = jnp.where(lax.axis_index(axis) == holder, block, jnp.zeros_like(block))
    return lax.psum(block, axis)


def product(left_mat, right_mat):
    return jnp.dot(
        left_mat, right_mat, precision=lax.Precision.HIGHEST, preferred_element_type=jnp.float32
    )


def orthonormal(gram_matrix, sketch):
    powered = product(gram_matrix, product(gram_matrix, sketch))
    chol_low = jnp.linalg.cholesky(product(powered.T, powered))
    return jax.scipy.linalg.solve_triangular(chol_low, powered.T, lower=True).T


def local(train_cores, sketch, exit_sketch):
    block_core = train_cores[0]
    full_rank = block_core.shape[0]
    mode_count = block_core.shape[1]
    kept_rank = sketch.shape[1]
    chain_len = lax.axis_size("cores")
    position = lax.axis_index("cores")
    vector_count = lax.axis_size("vec")
    identity = jnp.eye(full_rank, dtype=jnp.float32)
    zero_square = jnp.zeros((full_rank, full_rank), jnp.float32)
    row_major = block_core.reshape(full_rank * mode_count, full_rank)
    wide_core = block_core.reshape(full_rank, mode_count * full_rank)

    def forward_gram(lower_in):
        absorbed = product(lower_in.T, wide_core).reshape(full_rank * mode_count, full_rank)
        return product(absorbed.T, absorbed)

    def zero_gram(operand):
        return zero_square

    lower_prev = identity
    lower_own = identity
    gram_own = identity
    for link_index in range(chain_len):
        active = position == link_index
        partial_value = lax.cond(active, forward_gram, zero_gram, lower_prev)
        summed = jnp.where(active, lax.psum(partial_value, "row"), identity)
        factor = jnp.linalg.cholesky(summed)
        if link_index + 1 < chain_len:
            arrived = broadcast(factor, "cores", link_index)
            lower_prev = jnp.where(position == link_index + 1, arrived, lower_prev)
        lower_own = jnp.where(active, factor, lower_own)
        gram_own = jnp.where(active, summed, gram_own)
    is_last = position == chain_len - 1
    incoming = orthonormal(gram_own, exit_sketch)

    def right_map_of(incoming_frame):
        solved = jax.scipy.linalg.solve_triangular(lower_own, incoming_frame, lower=True, trans=1)
        return jnp.where(is_last, incoming_frame, solved)

    def backward_gram(incoming_frame):
        reduced = product(row_major, right_map_of(incoming_frame)).reshape(
            full_rank, mode_count * kept_rank
        )
        inner_gram = product(reduced, reduced.T)
        return product(lower_prev.T, product(inner_gram, lower_prev))

    frame_own = jnp.zeros((full_rank, kept_rank), jnp.float32)
    for link_index in range(chain_len):
        target = chain_len - 1 - link_index
        active = position == target
        partial_value = lax.cond(active, backward_gram, zero_gram, incoming)
        summed = jnp.where(active, lax.psum(partial_value, "row"), identity)
        frame = orthonormal(summed, sketch)
        if target > 0:
            arrived = broadcast(frame, "cores", target)
            incoming = jnp.where(position == target - 1, arrived, incoming)
        frame_own = jnp.where(active, frame, frame_own)
    reduced = product(row_major, right_map_of(incoming)).reshape(full_rank, mode_count * kept_rank)
    front_map = product(frame_own.T, lower_prev.T)
    shaped = product(front_map, reduced)
    rounded = (shaped * math.sqrt(kept_rank * MODE)).reshape(1, kept_rank, mode_count, kept_rank)
    bases_out = (frame_own * math.sqrt(full_rank))[None]
    gathered, frames_all = (
        lax.all_gather(shaped[None], "vec", axis=0, tiled=True),
        lax.all_gather(frame_own[None], "vec", axis=0, tiled=True),
    )
    start_env = jnp.einsum("az,qay->qzy", frame_own, frames_all, precision=lax.Precision.HIGHEST)
    mine_rows = shaped.reshape(kept_rank * mode_count, kept_rank)
    zero_env = jnp.zeros((vector_count, kept_rank, kept_rank), jnp.float32)

    def margin_terms(env_in):
        carried = jnp.einsum("qzw,qwx->qzx", env_in, gathered, precision=lax.Precision.HIGHEST)
        carried = carried.reshape(vector_count, kept_rank * mode_count, kept_rank)
        return jnp.einsum("cb,qcy->qby", mine_rows, carried, precision=lax.Precision.HIGHEST)

    def zero_margin(operand):
        return zero_env

    env_in = start_env
    env_own = zero_env
    for link_index in range(chain_len):
        active = position == link_index
        partial_value = lax.cond(active, margin_terms, zero_margin, env_in)
        summed = lax.psum(partial_value, "row")
        if link_index + 1 < chain_len:
            arrived = broadcast(summed, "cores", link_index)
            env_in = jnp.where(position == link_index + 1, arrived, env_in)
        env_own = jnp.where(active, summed, env_own)
    margins = env_own.transpose(1, 0, 2).reshape(kept_rank, vector_count * kept_rank)[None]
    return (rounded, bases_out, margins)


def solution(mesh):
    return jax.shard_map(
        local,
        mesh=mesh,
        in_specs=(P("vec", "cores", "row", None), P("cores", None), P()),
        out_specs=(
            P("vec", "cores", "row", None),
            P("vec", "cores", None),
            P("vec", "cores", None),
        ),
        check_vma=False,
    )
```

profile of v0, /device:TPU:0, one launch (start us, length us, event | category | flops | bytes accessed | tf_op | source)
XLA Modules:
  0.0 1274.4 jit_solution(12822136770054699126)
XLA Ops:
  7.3 18.5 %copy.85 = f32[32,8,64,256]{3,1,2,0:T(8,128)} copy(f32[32,8,64,256]{3,2,1,0:T(8,128)} %bitcast.211) | data formatting | bytes 33554432
  25.7 77.1 %conditional.6 = (f32[256,256]{1,0:T(8,128)S(1)}) conditional(s32[]{:T(128)} %convert_element_type.27, () %tuple.50, (f32[256,256]{0,1:T(8,128)S(1)}, f32[256,16384]{1,0:T(8,128)}) %tuple.167), branch_computations={%region_0.0_spmd, %region_1.0_spmd} | conditional | flops 25769803776 | bytes 84410376 | solution.py:52
  25.9 21.6 %fusion.102 = f32[256,16384]{1,0:T(8,128)} fusion(f32[256,256]{0,1:T(8,128)S(1)} %get-tuple-element.145, f32[256,16384]{1,0:T(8,128)} %get-tuple-element.62), kind=kOutput, calls=%fused_computation.165 | convolution fusion | flops 12884901888 | bytes 33816576 | tf_op jit(solution)/shard_map/cond/branch_1_fun/dot_general | solution.py:16
  47.5 18.0 %reshape.47 = f32[16384,256]{1,0:T(8,128)} reshape(f32[256,16384]{1,0:T(8,128)} %fusion.102) | data formatting | bytes 33554432 | tf_op jit(solution)/shard_map/cond/branch_1_fun/reshape | solution.py:41
  65.5 37.1 %fusion.103 = f32[256,256]{1,0:T(8,128)S(1)} fusion(f32[16384,256]{1,0:T(8,128)} %reshape.47), kind=kOutput, calls=%fused_computation.166 | convolution fusion | flops 12884901888 | bytes 17039360 | tf_op jit(solution)/shard_map/cond/branch_1_fun/dot_general | solution.py:16
  102.8 0.8 copy.43
  103.7 45.9 %all-reduce.11.cloned.1.call-done = f32[256,256]{0,1:T(8,128)} async-done(((f32[256,256]{0,1:T(8,128)}), f32[256,256]{0,1:T(8,128)}) %all-reduce.11.cloned.1.call-update) | async-done | bytes 262160 | tf_op jit(solution)/shard_map/psum | solution.py:53
  149.6 1.0 convert_select_fusion.6
  150.7 1.0 fusion.38
  151.8 11.7 cholesky.187
  163.6 9.8 custom-call.23
  174.0 11.7 cholesky.204
  188.7 18.3 %all-reduce.13.cloned.1.call-done = f32[256,256]{0,1:T(8,128)} async-done(((f32[256,256]{0,1:T(8,128)}), f32[256,256]{0,1:T(8,128)}) %all-reduce.13.cloned.1.call-update) | async-done | bytes 262160 | tf_op jit(solution)/shard_map/psum | solution.py:12
  207.0 8.9 conditional.7
  216.0 0.8 copy.49
  216.9 113.5 %all-reduce.15.cloned.1.call-done = f32[256,256]{0,1:T(8,128)} async-done(((f32[256,256]{0,1:T(8,128)}), f32[256,256]{0,1:T(8,128)}) %all-reduce.15.cloned.1.call-update) | async-done | bytes 262160 | tf_op jit(solution)/shard_map/psum | solution.py:53
  330.6 11.7 cholesky.221
  342.5 9.8 custom-call.24
  352.9 11.7 cholesky.238
  366.5 11.9 cholesky.253
  379.7 9.8 custom-call.25
  392.5 8.0 conditional.8
  401.4 116.7 %all-reduce.17.cloned.1.call-done = f32[256,256]{0,1:T(8,128)} async-done(((f32[256,256]{0,1:T(8,128)}), f32[256,256]{0,1:T(8,128)}) %all-reduce.17.cloned.1.call-update) | async-done | bytes 262160 | tf_op jit(solution)/shard_map/psum | solution.py:79
  519.8 11.7 cholesky.264
  532.8 9.8 custom-call.26
  542.6 1.0 fusion.32
  543.8 4.2 while.8
  544.4 1.4 dynamic-slice.19
  546.5 1.4 dynamic-slice.19
  547.9 19.7 %custom-call.28 = f32[2,128,128]{1,2,0:T(8,128)S(1)} custom-call(f32[2,128,128]{2,1,0:T(8,128)S(1)} %get-tuple-element.115), custom_call_target="InvertDiagBlocksLowerTriangular" | custom-call | tf_op jit(solution)/shard_map/jit(_solve_triangular)/triangular_solve | solution.py:64
  567.7 0.9 broadcast_select_fusion.2
  569.3 78.2 %conditional.9 = (f32[256,256]{0,1:T(8,128)S(1)}) conditional(s32[]{:T(128)} %convert_element_type.27, () %tuple.48, (pred[]{:T(512)}, f32[256,256]{0,1:T(8,128)S(1)}, f32[256,128]{0,1:T(8,128)S(1)}, f32[16384,256]{1,0:T(8,128)}, f32[256,256]{0,1:T(8,128)S(1)}) %tuple.166), branch_computations={%region_17.22_spmd, %region_18.23_spmd} | conditional | flops 13363265536 | bytes 71303368 | solution.py:78
  569.8 4.0 while.7
  570.4 1.4 bitcast_dynamic-update-slice_fusion.7
  572.4 1.4 bitcast_dynamic-update-slice_fusion.7
  573.8 19.7 %custom-call.22 = f32[2,128,128]{1,2,0:T(8,128)S(1)} custom-call(f32[2,128,128]{2,1,0:T(8,128)S(1)} %get-tuple-element.114), custom_call_target="InvertDiagBlocksLowerTriangular" | custom-call | tf_op jit(solution)/shard_map/cond/branch_1_fun/jit(_solve_triangular)/triangular_solve | solution.py:64
  594.2 23.1 %convolution_bitcast_fusion.2 = f32[16384,128]{0,1:T(8,128)} fusion(f32[16384,256]{1,0:T(8,128)} %get-tuple-element.80, f32[256,128]{1,0:T(8,128)S(1)} %copy.60, f32[128,128]{1,0:T(8,128)S(1)} %fusion.25, f32[128,128]{1,0:T(8,128)S(1)} %fusion.28, pred[]{:T(512)} %get-tuple-element.77), kind=kOutput, calls=%fused_computation.30 | convolution fusion | flops 6442516480 | bytes 25427968 | tf_op jit(solution)/shard_map/cond/branch_1_fun/dot_general | solution.py:16
  617.2 9.0 copy.41
  626.2 9.4 reshape.50
  635.6 10.6 fusion.109
  648.5 22.4 %convolution_bitcast_fusion.4 = f32[16384,128]{0,1:T(8,128)} fusion(f32[16384,256]{1,0:T(8,128)} %bitcast.214, f32[256,128]{0,1:T(8,128)S(1)} %broadcast_select_fusion.2, f32[128,128]{0,1:T(8,128)S(1)} %copy.64, f32[128,128]{0,1:T(8,128)S(1)} %fusion.67, pred[]{:T(512)} %eq.35), kind=kOutput, calls=%fused_computation.49 | convolution fusion | flops 6442516480 | bytes 25427968 | tf_op jit(solution)/shard_map/dot_general | solution.py:16
  670.9 9.0 copy.65
  680.0 9.8 reshape.56
  689.8 1.6 all-reduce.21.cloned.1.call-done
  691.4 1.5 fusion.45
  692.9 1.6 fusion.44
  695.0 11.7 cholesky.275
  708.0 9.8 custom-call.27
  718.5 10.4 fusion.115
  728.9 4.9 reshape.58
  733.8 19.3 %all-gather = f32[1024,128]{0,1:T(8,128)S(1)} all-gather(f32[256,128]{0,1:T(8,128)S(1)} %fusion.31), channel_id=2, replica_groups=mesh['cores'=2,'row'=4,'vec'=4] {'vec'}, dimensions={0}, use_global_device_ids=true | all-gather | bytes 655360 | tf_op jit(solution)/shard_map/all_gather | solution.py:92
  753.7 264.3 %all-gather.4.cloned.1.call-done = f32[512,8192]{1,0:T(8,128)} async-done(((f32[128,8192]{1,0:T(8,128)}), f32[512,8192]{1,0:T(8,128)}) %all-gather.4.cloned.1.call-update) | async-done | bytes 16777232 | tf_op jit(solution)/shard_map/all_gather | solution.py:91
  1018.0 69.0 %conditional.10 = (f32[4,128,128]{1,2,0:T(8,128)S(1)}) conditional(s32[]{:T(128)} %convert_element_type.27, () %tuple.57, (f32[4,128,128]{1,2,0:T(8,128)S(1)}, f32[4,128,8192]{2,1,0:T(8,128)}, f32[8192,128]{1,0:T(8,128)}) %tuple.169), branch_computations={%region_20.25_spmd, %region_21.26_spmd} | conditional | flops 12884901888 | bytes 88604680 | solution.py:110
  1018.0 21.6 %fusion.106 = f32[4,128,8192]{2,1,0:T(8,128)} fusion(f32[4,128,128]{1,2,0:T(8,128)S(1)} %get-tuple-element.163, f32[4,128,8192]{2,1,0:T(8,128)} %get-tuple-element.83), kind=kOutput, calls=%fused_computation.169 | convolution fusion | flops 6442450944 | bytes 33816576 | tf_op jit(solution)/shard_map/cond/branch_1_fun/qzw,qwx->qzx/dot_general | solution.py:99
  1039.6 18.0 %reshape.51 = f32[4,8192,128]{2,1,0:T(8,128)} reshape(f32[4,128,8192]{2,1,0:T(8,128)} %fusion.106) | data formatting | bytes 33554432 | tf_op jit(solution)/shard_map/cond/branch_1_fun/reshape | solution.py:100
  1057.6 29.2 %fusion.2 = f32[4,128,128]{1,2,0:T(8,128)S(1)} fusion(f32[4,8192,128]{2,1,0:T(8,128)} %reshape.51, f32[8192,128]{1,0:T(8,128)} %get-tuple-element.84), kind=kOutput, calls=%fused_computation.2 | convolution fusion | flops 6442450944 | bytes 21233664 | tf_op jit(solution)/shard_map/cond/branch_1_fun/cb,qcy->qby/dot_general | solution.py:101
  1087.8 41.6 %all-reduce.23.cloned.1.call-done = f32[4,128,128]{1,2,0:T(8,128)} async-done(((f32[4,128,128]{1,2,0:T(8,128)}), f32[4,128,128]{1,2,0:T(8,128)}) %all-reduce.23.cloned.1.call-update) | async-done | bytes 262160 | tf_op jit(solution)/shard_map/psum | solution.py:111
  1129.4 1.7 broadcast_select_fusion
  1131.9 18.6 %all-reduce.25.cloned.1.call-done = f32[4,128,128]{1,2,0:T(8,128)} async-done(((f32[4,128,128]{1,2,0:T(8,128)}), f32[4,128,128]{1,2,0:T(8,128)}) %all-reduce.25.cloned.1.call-update) | async-done | bytes 262160 | tf_op jit(solution)/shard_map/psum | solution.py:12
  1150.5 2.0 conditional.11
  1153.3 2.6 multiply_bitcast_fusion
  1155.8 2.8 copy.86
  1158.6 107.6 %all-reduce.27.cloned.1.call-done = f32[4,128,128]{1,2,0:T(8,128)} async-done(((f32[4,128,128]{1,2,0:T(8,128)}), f32[4,128,128]{1,2,0:T(8,128)}) %all-reduce.27.cloned.1.call-update) | async-done | bytes 262160 | tf_op jit(solution)/shard_map/psum | solution.py:111
  1266.2 0.8 copy.82
  (134 shorter events, 24.0 us)
Async XLA Ops:
  7.2 510.9 %copy-start = (f32[256,128]{1,0:T(8,128)S(1)}, f32[256,128]{1,0:T(8,128)}, u32[]{:S(2)}) copy-start(f32[256,128]{1,0:T(8,128)} %param.22) | copy-start | bytes 393220
  7.2 142.4 %all-reduce.11.cloned.1.call-start = ((), (), s32[]{:S(2)}) async-start(), calls=%async_computation | async-start | bytes 524288 | tf_op jit(solution)/shard_map/psum | solution.py:53
  103.7 103.3 %all-reduce.13.cloned.1.call-start = ((), (), s32[]{:S(2)}) async-start(), calls=%async_computation.1 | async-start | bytes 524288 | tf_op jit(solution)/shard_map/psum | solution.py:12
  188.6 141.8 %all-reduce.15.cloned.1.call-start = ((), (), s32[]{:S(2)}) async-start(), calls=%async_computation.2 | async-start | bytes 524288 | tf_op jit(solution)/shard_map/psum | solution.py:53
  207.0 157.7 %copy-start.1 = (f32[256,256]{0,1:T(8,128)S(1)}, f32[256,256]{0,1:T(8,128)}, u32[]{:S(2)}) copy-start(f32[256,256]{0,1:T(8,128)} %all-reduce.11.cloned.1.call-done) | copy-start | bytes 786436
  207.0 157.7 %copy-start.8 = (f32[256,128]{1,0:T(8,128)S(1)}, f32[256,128]{1,0:T(8,128)}, u32[]{:S(2)}) copy-start(f32[256,128]{1,0:T(8,128)} %param.23) | copy-start | bytes 393220
  216.9 301.2 %all-reduce.17.cloned.1.call-start = ((), (), s32[]{:S(2)}) async-start(), calls=%async_computation.3 | async-start | bytes 524288 | tf_op jit(solution)/shard_map/psum | solution.py:79
  400.6 0.7 copy-start.4
  401.3 166.3 %all-reduce.19.cloned.1.call-start = ((), (), s32[]{:S(2)}) async-start(), calls=%async_computation.4 | async-start | bytes 262144 | tf_op jit(solution)/shard_map/psum | solution.py:12
  543.6 147.7 %all-reduce.21.cloned.1.call-start = ((), (), s32[]{:S(2)}) async-start(), calls=%async_computation.5 | async-start | bytes 524288 | tf_op jit(solution)/shard_map/psum | solution.py:79
  647.5 0.7 copy-start.5
  648.2 369.9 %all-gather.4.cloned.1.call-start = ((), (), s32[]{:S(2)}) async-start(), calls=%async_computation.9 | async-start | bytes 20971520 | tf_op jit(solution)/shard_map/all_gather | solution.py:91
  670.9 46.9 %copy-start.2 = (f32[256,128]{0,1:T(8,128)S(1)}, f32[256,128]{0,1:T(8,128)}, u32[]{:S(2)}) copy-start(f32[256,128]{0,1:T(8,128)} %fusion.32) | copy-start | bytes 393220
  728.9 400.5 %all-reduce.23.cloned.1.call-start = ((), (), s32[]{:S(2)}) async-start(), calls=%async_computation.6 | async-start | bytes 524288 | tf_op jit(solution)/shard_map/psum | solution.py:111
  1087.0 0.7 copy-start.6
  1087.8 62.8 %all-reduce.25.cloned.1.call-start = ((), (), s32[]{:S(2)}) async-start(), calls=%async_computation.7 | async-start | bytes 524288 | tf_op jit(solution)/shard_map/psum | solution.py:12
  1131.1 135.1 %all-reduce.27.cloned.1.call-start = ((), (), s32[]{:S(2)}) async-start(), calls=%async_computation.8 | async-start | bytes 524288 | tf_op jit(solution)/shard_map/psum | solution.py:111
  1152.5 0.7 copy-start.7
  1152.5 113.6 %copy-start.3 = (f32[4,128,128]{1,2,0:T(8,128)S(1)}, f32[4,128,128]{1,2,0:T(8,128)}, u32[]{:S(2)}) copy-start(f32[4,128,128]{1,2,0:T(8,128)} %all-reduce.23.cloned.1.call-done) | copy-start | bytes 786436
Sparse Core Ops, SparseCore 0:
  103.8 45.7 all-reduce.10
  188.7 18.1 all-reduce.12
  217.0 113.3 all-reduce.14
  401.4 116.5 all-reduce.16
  543.8 19.1 all-reduce.18
  648.3 43.0 all-reduce.20
  729.0 289.0 all-gather.3
  1087.9 41.4 all-reduce.22
  1132.3 18.2 all-reduce.24
  1153.9 112.2 all-reduce.26
where the time goes:
time: 1280 us; the launch traced here: 1270 us
  waiting for transfers between devices  728 us (57%)
  matrix products  189 us (15%)
  other arithmetic  185 us (14%)
  local copies, waits for them, and re-layouts  115 us (9%)
  loops' own time  20.1 us (2%)
  blocking collectives  19.3 us (2%)
  between operations  17.9 us (1%)
    psum x4, waiting for transfers between devices, local(): summed = jnp.where(active, lax.psum(partial_value, 'row'), identity)  278 us
    all_gather x1, waiting for transfers between devices, local(): lax.all_gather(shaped[None], 'vec', axis=0, tiled=True)  264 us
    psum x2, waiting for transfers between devices, local(): summed = lax.psum(partial_value, 'row')  149 us
    dot_general x18, matrix products, product(): jnp.dot(left_mat, right_mat, precision=lax.Precision.HIGHEST, preferred_e...  133 us
    another operation x13, other arithmetic, local(): factor = jnp.linalg.cholesky(summed)  68.5 us
    another operation x8, other arithmetic, right_map_of(): jax.scipy.linalg.solve_triangular(lower_own, incoming_frame, lower=True,...  39.4 us
    another operation x9, other arithmetic, orthonormal(): chol_low = jnp.linalg.cholesky(product(powered.T, powered))  37.3 us
    psum x3, waiting for transfers between devices, broadcast(): return lax.psum(block, axis)  37 us
  transfers between devices with their start and end apart: 10, of which 9 were waited for; matrix products, arithmetic and copies ran while one was open for 6% of the time, Pallas kernels for 0%

commit v1 on v0

--- a/solution.py
+++ b/solution.py
@@ -5,6 +5,12 @@
 from jax.sharding import PartitionSpec as P
 
 MODE = 256
+
+
+def tiled_gather(x, axis, dim):
+    size = lax.axis_size(axis)
+    repeats = [size if d == dim else 1 for d in range(x.ndim)]
+    return lax.all_to_all(jnp.tile(x, repeats), axis, split_axis=dim, concat_axis=dim, tiled=True)
 
 
 def broadcast(block, axis, holder):
@@ -88,7 +94,7 @@
     rounded = (shaped * math.sqrt(kept_rank * MODE)).reshape(1, kept_rank, mode_count, kept_rank)
     bases_out = (frame_own * math.sqrt(full_rank))[None]
     gathered, frames_all = (
-        lax.all_gather(shaped[None], "vec", axis=0, tiled=True),
+        tiled_gather(shaped[None], "vec", 0),
         lax.all_gather(frame_own[None], "vec", axis=0, tiled=True),
     )
     start_env = jnp.einsum("az,qay->qzy", frame_own, frames_all, precision=lax.Precision.HIGHEST)

time: 1280 us -> 1390 us (1.086)
  blocking collectives: 19.3 us -> 366 us
  waiting for transfers between devices: 728 us -> 465 us
    all_gather x1, blocking collectives: 19.3 us -> 366 us  [local(): lax.all_gather(frame_own[None], 'vec', axis=0, tiled=True)]
    all_gather x1 -> x0, waiting for transfers between devices: 264 us -> none  [local(): lax.all_gather(shaped[None], 'vec', axis=0, tiled=True)]
  transfers between devices with their start and end apart: 10 -> 10, of which waited for: 9 -> 8; matrix products, arithmetic and copies ran while one was open for 6% -> 6% of each run, Pallas kernels for 0% -> 0%
where the time goes in v1:
time: 1390 us; the launch traced here: 1380 us
  waiting for transfers between devices  465 us (33%)
  blocking collectives  366 us (26%)
  other arithmetic  185 us (13%)
  matrix products  185 us (13%)
  local copies, waits for them, and re-layouts  125 us (9%)
  loops' own time  30.7 us (2%)
  between operations  17.4 us (1%)
    all_gather x1, blocking collectives, local(): lax.all_gather(frame_own[None], 'vec', axis=0, tiled=True)  366 us
    psum x4, waiting for transfers between devices, local(): summed = jnp.where(active, lax.psum(partial_value, 'row'), identity)  278 us
    psum x2, waiting for transfers between devices, local(): summed = lax.psum(partial_value, 'row')  151 us
    dot_general x18, matrix products, product(): jnp.dot(left_mat, right_mat, precision=lax.Precision.HIGHEST, preferred_e...  130 us
    another operation x13, other arithmetic, local(): factor = jnp.linalg.cholesky(summed)  68.5 us
    another operation x8, other arithmetic, right_map_of(): jax.scipy.linalg.solve_triangular(lower_own, incoming_frame, lower=True,...  39.4 us
    another operation x9, other arithmetic, orthonormal(): chol_low = jnp.linalg.cholesky(product(powered.T, powered))  37.6 us
    psum x3, waiting for transfers between devices, broadcast(): return lax.psum(block, axis)  37 us
  transfers between devices with their start and end apart: 10, of which 8 were waited for; matrix products, arithmetic and copies ran while one was open for 6% of the time, Pallas kernels for 0%

profile of v1, /device:TPU:0, one launch (start us, length us, event | category | flops | bytes accessed | tf_op | source)
XLA Modules:
  0.0 1381.9 jit_solution(12226629905804331857)
XLA Ops:
  7.3 18.5 %copy.85 = f32[32,8,64,256]{3,1,2,0:T(8,128)} copy(f32[32,8,64,256]{3,2,1,0:T(8,128)} %bitcast.210) | data formatting | bytes 33554432
  25.7 77.1 %conditional.6 = (f32[256,256]{1,0:T(8,128)S(1)}) conditional(s32[]{:T(128)} %convert_element_type.27, () %tuple.50, (f32[256,256]{0,1:T(8,128)S(1)}, f32[256,16384]{1,0:T(8,128)}) %tuple.165), branch_computations={%region_0.0_spmd, %region_1.0_spmd} | conditional | flops 25769803776 | bytes 84410376 | solution.py:58
  25.9 21.6 %fusion.102 = f32[256,16384]{1,0:T(8,128)} fusion(f32[256,256]{0,1:T(8,128)S(1)} %get-tuple-element.145, f32[256,16384]{1,0:T(8,128)} %get-tuple-element.62), kind=kOutput, calls=%fused_computation.165 | convolution fusion | flops 12884901888 | bytes 33816576 | tf_op jit(solution)/shard_map/cond/branch_1_fun/dot_general | solution.py:22
  47.5 18.0 %reshape.50 = f32[16384,256]{1,0:T(8,128)} reshape(f32[256,16384]{1,0:T(8,128)} %fusion.102) | data formatting | bytes 33554432 | tf_op jit(solution)/shard_map/cond/branch_1_fun/reshape | solution.py:47
  65.5 36.9 %fusion.103 = f32[256,256]{1,0:T(8,128)S(1)} fusion(f32[16384,256]{1,0:T(8,128)} %reshape.50), kind=kOutput, calls=%fused_computation.166 | convolution fusion | flops 12884901888 | bytes 17039360 | tf_op jit(solution)/shard_map/cond/branch_1_fun/dot_general | solution.py:22
  102.8 0.8 copy.43
  103.7 45.9 %all-reduce.11.cloned.1.call-done = f32[256,256]{0,1:T(8,128)} async-done(((f32[256,256]{0,1:T(8,128)}), f32[256,256]{0,1:T(8,128)}) %all-reduce.11.cloned.1.call-update) | async-done | bytes 262160 | tf_op jit(solution)/shard_map/psum | solution.py:59
  149.6 1.0 convert_select_fusion.6
  150.7 1.0 fusion.38
  151.8 11.7 cholesky.187
  163.6 9.8 custom-call.23
  174.0 11.7 cholesky.204
  188.7 18.3 %all-reduce.13.cloned.1.call-done = f32[256,256]{0,1:T(8,128)} async-done(((f32[256,256]{0,1:T(8,128)}), f32[256,256]{0,1:T(8,128)}) %all-reduce.13.cloned.1.call-update) | async-done | bytes 262160 | tf_op jit(solution)/shard_map/psum | solution.py:18
  207.0 8.7 conditional.7
  216.7 113.6 %all-reduce.15.cloned.1.call-done = f32[256,256]{0,1:T(8,128)} async-done(((f32[256,256]{0,1:T(8,128)}), f32[256,256]{0,1:T(8,128)}) %all-reduce.15.cloned.1.call-update) | async-done | bytes 262160 | tf_op jit(solution)/shard_map/psum | solution.py:59
  330.6 11.7 cholesky.221
  342.4 9.8 custom-call.24
  352.8 11.7 cholesky.238
  366.4 12.1 cholesky.253
  379.9 9.8 custom-call.25
  392.7 7.9 conditional.8
  401.4 116.6 %all-reduce.17.cloned.1.call-done = f32[256,256]{0,1:T(8,128)} async-done(((f32[256,256]{0,1:T(8,128)}), f32[256,256]{0,1:T(8,128)}) %all-reduce.17.cloned.1.call-update) | async-done | bytes 262160 | tf_op jit(solution)/shard_map/psum | solution.py:85
  519.7 11.7 cholesky.264
  532.8 9.8 custom-call.26
  542.6 1.0 fusion.32
  543.7 4.2 while.8
  544.3 1.4 dynamic-slice.19
  546.4 1.4 dynamic-slice.19
  547.9 19.7 %custom-call.28 = f32[2,128,128]{1,2,0:T(8,128)S(1)} custom-call(f32[2,128,128]{2,1,0:T(8,128)S(1)} %get-tuple-element.115), custom_call_target="InvertDiagBlocksLowerTriangular" | custom-call | tf_op jit(solution)/shard_map/jit(_solve_triangular)/triangular_solve | solution.py:70
  567.6 0.9 broadcast_select_fusion.2
  569.2 88.9 %conditional.9 = (f32[256,256]{0,1:T(8,128)S(1)}) conditional(s32[]{:T(128)} %convert_element_type.27, () %tuple.48, (pred[]{:T(512)}, f32[256,256]{0,1:T(8,128)S(1)}, f32[256,128]{0,1:T(8,128)S(1)}, f32[16384,256]{1,0:T(8,128)}, f32[256,256]{0,1:T(8,128)S(1)}) %tuple.164), branch_computations={%region_17.22_spmd, %region_18.23_spmd} | conditional | flops 13363265536 | bytes 71303368 | solution.py:84
  580.4 4.0 while.7
  581.0 1.4 bitcast_dynamic-update-slice_fusion.7
  583.0 1.4 bitcast_dynamic-update-slice_fusion.7
  584.4 19.7 %custom-call.22 = f32[2,128,128]{1,2,0:T(8,128)S(1)} custom-call(f32[2,128,128]{2,1,0:T(8,128)S(1)} %get-tuple-element.114), custom_call_target="InvertDiagBlocksLowerTriangular" | custom-call | tf_op jit(solution)/shard_map/cond/branch_1_fun/jit(_solve_triangular)/triangular_solve | solution.py:70
  604.8 23.1 %convolution_bitcast_fusion.2 = f32[16384,128]{0,1:T(8,128)} fusion(f32[16384,256]{1,0:T(8,128)} %get-tuple-element.80, f32[256,128]{1,0:T(8,128)S(1)} %copy.60, f32[128,128]{1,0:T(8,128)S(1)} %fusion.25, f32[128,128]{1,0:T(8,128)S(1)} %fusion.28, pred[]{:T(512)} %get-tuple-element.77), kind=kOutput, calls=%fused_computation.30 | convolution fusion | flops 6442516480 | bytes 25427968 | tf_op jit(solution)/shard_map/cond/branch_1_fun/dot_general | solution.py:22
  627.9 9.0 copy.41
  636.9 9.4 reshape.53
  646.3 10.6 fusion.109
  659.1 22.4 %convolution_bitcast_fusion.4 = f32[16384,128]{0,1:T(8,128)} fusion(f32[16384,256]{1,0:T(8,128)} %bitcast.213, f32[256,128]{0,1:T(8,128)S(1)} %broadcast_select_fusion.2, f32[128,128]{0,1:T(8,128)S(1)} %copy.64, f32[128,128]{0,1:T(8,128)S(1)} %fusion.67, pred[]{:T(512)} %eq.35), kind=kOutput, calls=%fused_computation.49 | convolution fusion | flops 6442516480 | bytes 25427968 | tf_op jit(solution)/shard_map/dot_general | solution.py:22
  681.5 9.0 copy.65
  690.6 9.8 reshape.59
  700.4 1.6 all-reduce.21.cloned.1.call-done
  702.0 1.5 fusion.45
  703.6 1.6 fusion.44
  705.6 11.7 cholesky.275
  718.7 9.8 custom-call.27
  729.1 6.9 fusion.115
  736.1 2.0 copy-done.1
  738.1 7.7 tile.2
  745.8 7.0 all-to-all-start
  752.8 5.1 reshape.61
  757.9 366.0 %all-gather = f32[1024,128]{0,1:T(8,128)S(1)} all-gather(f32[256,128]{0,1:T(8,128)S(1)} %fusion.31), channel_id=2, replica_groups=mesh['cores'=2,'row'=4,'vec'=4] {'vec'}, dimensions={0}, use_global_device_ids=true | all-gather | bytes 655360 | tf_op jit(solution)/shard_map/all_gather | solution.py:98
  1124.5 69.0 %conditional.10 = (f32[4,128,128]{1,2,0:T(8,128)S(1)}) conditional(s32[]{:T(128)} %convert_element_type.27, () %tuple.57, (f32[4,128,128]{1,2,0:T(8,128)S(1)}, f32[4,128,8192]{2,1,0:T(8,128)}, f32[8192,128]{1,0:T(8,128)}) %tuple.58), branch_computations={%region_20.25_spmd, %region_21.26_spmd} | conditional | flops 12884901888 | bytes 88604680 | solution.py:116
  1124.5 21.6 %fusion.106 = f32[4,128,8192]{2,1,0:T(8,128)} fusion(f32[4,128,128]{1,2,0:T(8,128)S(1)} %get-tuple-element.163, f32[4,128,8192]{2,1,0:T(8,128)} %get-tuple-element.83), kind=kOutput, calls=%fused_computation.169 | convolution fusion | flops 6442450944 | bytes 33816576 | tf_op jit(solution)/shard_map/cond/branch_1_fun/qzw,qwx->qzx/dot_general | solution.py:105
  1146.1 18.0 %reshape.54 = f32[4,8192,128]{2,1,0:T(8,128)} reshape(f32[4,128,8192]{2,1,0:T(8,128)} %fusion.106) | data formatting | bytes 33554432 | tf_op jit(solution)/shard_map/cond/branch_1_fun/reshape | solution.py:106
  1164.1 29.2 %fusion.2 = f32[4,128,128]{1,2,0:T(8,128)S(1)} fusion(f32[4,8192,128]{2,1,0:T(8,128)} %reshape.54, f32[8192,128]{1,0:T(8,128)} %get-tuple-element.84), kind=kOutput, calls=%fused_computation.2 | convolution fusion | flops 6442450944 | bytes 21233664 | tf_op jit(solution)/shard_map/cond/branch_1_fun/cb,qcy->qby/dot_general | solution.py:107
  1194.3 43.1 %all-reduce.23.cloned.1.call-done = f32[4,128,128]{1,2,0:T(8,128)} async-done(((f32[4,128,128]{1,2,0:T(8,128)}), f32[4,128,128]{1,2,0:T(8,128)}) %all-reduce.23.cloned.1.call-update) | async-done | bytes 262160 | tf_op jit(solution)/shard_map/psum | solution.py:117
  1237.4 1.7 broadcast_select_fusion
  1239.9 18.6 %all-reduce.25.cloned.1.call-done = f32[4,128,128]{1,2,0:T(8,128)} async-done(((f32[4,128,128]{1,2,0:T(8,128)}), f32[4,128,128]{1,2,0:T(8,128)}) %all-reduce.25.cloned.1.call-update) | async-done | bytes 262160 | tf_op jit(solution)/shard_map/psum | solution.py:18
  1258.5 2.0 conditional.11
  1261.3 2.6 multiply_bitcast_fusion
  1263.8 2.8 copy.86
  1266.6 107.6 %all-reduce.27.cloned.1.call-done = f32[4,128,128]{1,2,0:T(8,128)} async-done(((f32[4,128,128]{1,2,0:T(8,128)}), f32[4,128,128]{1,2,0:T(8,128)}) %all-reduce.27.cloned.1.call-update) | async-done | bytes 262160 | tf_op jit(solution)/shard_map/psum | solution.py:117
  (136 shorter events, 25.6 us)
Async XLA Ops:
  7.2 510.8 %copy-start = (f32[256,128]{1,0:T(8,128)S(1)}, f32[256,128]{1,0:T(8,128)}, u32[]{:S(2)}) copy-start(f32[256,128]{1,0:T(8,128)} %param.22) | copy-start | bytes 393220
  7.2 142.4 %all-reduce.11.cloned.1.call-start = ((), (), s32[]{:S(2)}) async-start(), calls=%async_computation.1 | async-start | bytes 524288 | tf_op jit(solution)/shard_map/psum | solution.py:59
  103.7 103.3 %all-reduce.13.cloned.1.call-start = ((), (), s32[]{:S(2)}) async-start(), calls=%async_computation.2 | async-start | bytes 524288 | tf_op jit(solution)/shard_map/psum | solution.py:18
  188.6 141.7 %all-reduce.15.cloned.1.call-start = ((), (), s32[]{:S(2)}) async-start(), calls=%async_computation.3 | async-start | bytes 524288 | tf_op jit(solution)/shard_map/psum | solution.py:59
  207.0 157.7 %copy-start.2 = (f32[256,256]{0,1:T(8,128)S(1)}, f32[256,256]{0,1:T(8,128)}, u32[]{:S(2)}) copy-start(f32[256,256]{0,1:T(8,128)} %all-reduce.11.cloned.1.call-done) | copy-start | bytes 786436
  207.0 157.7 %copy-start.9 = (f32[256,128]{1,0:T(8,128)S(1)}, f32[256,128]{1,0:T(8,128)}, u32[]{:S(2)}) copy-start(f32[256,128]{1,0:T(8,128)} %param.23) | copy-start | bytes 393220
  216.7 301.3 %all-reduce.17.cloned.1.call-start = ((), (), s32[]{:S(2)}) async-start(), calls=%async_computation.4 | async-start | bytes 524288 | tf_op jit(solution)/shard_map/psum | solution.py:85
  400.6 0.7 copy-start.5
  401.3 166.2 %all-reduce.19.cloned.1.call-start = ((), (), s32[]{:S(2)}) async-start(), calls=%async_computation.5 | async-start | bytes 262144 | tf_op jit(solution)/shard_map/psum | solution.py:18
  543.6 158.4 %all-reduce.21.cloned.1.call-start = ((), (), s32[]{:S(2)}) async-start(), calls=%async_computation.6 | async-start | bytes 524288 | tf_op jit(solution)/shard_map/psum | solution.py:85
  658.1 0.7 copy-start.6
  681.5 47.0 %copy-start.3 = (f32[256,128]{0,1:T(8,128)S(1)}, f32[256,128]{0,1:T(8,128)}, u32[]{:S(2)}) copy-start(f32[256,128]{0,1:T(8,128)} %fusion.32) | copy-start | bytes 393220
  736.0 2.0 copy-start.1
  745.8 378.7 %all-to-all-start = ((f32[4,128,8192]{2,1,0:T(8,128)}), f32[4,128,8192]{2,1,0:T(8,128)}, u32[]{:S(2)}, u32[]{:S(2)}) async-start(f32[4,128,8192]{2,1,0:T(8,128)} %tile.2), calls=%async_computation | async-start | bytes 33554432 | tf_op jit(solution)/shard_map/all_to_all | solution.py:13
  752.8 484.6 %all-reduce.23.cloned.1.call-start = ((), (), s32[]{:S(2)}) async-start(), calls=%async_computation.7 | async-start | bytes 524288 | tf_op jit(solution)/shard_map/psum | solution.py:117
  1193.5 0.7 copy-start.7
  1194.3 64.3 %all-reduce.25.cloned.1.call-start = ((), (), s32[]{:S(2)}) async-start(), calls=%async_computation.8 | async-start | bytes 524288 | tf_op jit(solution)/shard_map/psum | solution.py:18
  1239.1 135.1 %all-reduce.27.cloned.1.call-start = ((), (), s32[]{:S(2)}) async-start(), calls=%async_computation.9 | async-start | bytes 524288 | tf_op jit(solution)/shard_map/psum | solution.py:117
  1260.5 0.7 copy-start.8
  1260.6 113.6 %copy-start.4 = (f32[4,128,128]{1,2,0:T(8,128)S(1)}, f32[4,128,128]{1,2,0:T(8,128)}, u32[]{:S(2)}) copy-start(f32[4,128,128]{1,2,0:T(8,128)} %all-reduce.23.cloned.1.call-done) | copy-start | bytes 786436
Sparse Core Ops, SparseCore 0:
  103.8 45.7 all-reduce.10
  188.7 18.2 all-reduce.12
  216.8 113.5 all-reduce.14
  401.5 116.4 all-reduce.16
  543.7 18.9 all-reduce.18
  658.9 43.0 all-reduce.20
  1194.4 42.9 all-reduce.22
  1240.3 18.2 all-reduce.24
  1262.0 112.0 all-reduce.26
